TPU v7x, 512 devices: a whole 4x8x8 slice. The times are simulated.
512 devices in a mesh: context: 8 (over z), expert: 32 (over x, y), dp: 2 (over core).
Axes of the slice: x: 4, y: 8, z: 8, core: 2. Of those that a mesh axis runs over, the one named last changes fastest.
Arguments:
- residual: bfloat16 [32768, 1024], P(('dp', 'expert', 'context')), parts along dimension 0, may hold values from -6 to 6
- queries: bfloat16 [32768, 2048], P(('dp', 'expert', 'context')), parts along dimension 0, may hold values from -4.6 to 4.6
- key_vectors: bfloat16 [32768, 256], P(('dp', 'expert', 'context')), parts along dimension 0, may hold values from -5 to 5
- value_vectors: bfloat16 [32768, 256], P(('dp', 'expert', 'context')), parts along dimension 0, may hold values from -5 to 5
- output_weight: bfloat16 [2048, 1024], P('context'), may hold values from -0.875 to 0.875
- norm_gain: float32 [1024], replicated, may hold values from 0.1 to 1.9
- routes: int32 [32768, 8], P(('dp', 'expert', 'context')), parts along dimension 0, may hold values from 0 to 127, all different within a row; in each aligned block of 64 rows (0 to 63, 64 to 127, ...) at most 5 rows name the same one
- gate_levels: int32 [32768, 8], P(('dp', 'expert', 'context')), parts along dimension 0, may hold values from 16 to 96
- expert_in: bfloat16 [256, 1024, 384], P(('context', 'expert')), may hold values from -0.1875 to 0.1875
- expert_out: bfloat16 [256, 192, 1024], P(('context', 'expert')), may hold values from -0.3125 to 0.3125
Outputs:
- layer_out: float32 [32768, 1024], P(('dp', 'expert', 'context')), parts along dimension 0
There are 2 independent parts, one for each index of `dp`. A program takes and returns all parts, laid end to end along the dimension named above; an argument that names none is the same for every part. Nothing has to cross between parts.
Inputs may be any that keep to these rules, and one draw needn't show every extreme that they name: `routes`: in the rows of one device no expert is named more than 5 times, and in every draw some expert reaches 5 in some device's rows; each row names 8 different experts.
All inputs are finite; a program needn't handle non-finite values.
Results may differ from a plain program's by a relative error of at most 0.022.
Values may be sent and summed in bfloat16 or wider, within the bound.
No kernel may reach another device: no remote copies, remote signals or barrier semaphores. Data moves between devices by JAX's collectives and lax.ppermute only.
A program may use at most 192 MiB of HBM per device.

v0:
```python
import math
import jax
import jax.numpy as jnp
import numpy as np
from jax import lax
from jax.sharding import PartitionSpec as P

HD = 128


def expert_apply(gathered, weight_in, weight_out):
    projection = jnp.dot(gathered, weight_in, preferred_element_type=jnp.float32)
    inner_half = weight_in.shape[1] // 2
    activated = (jax.nn.silu(projection[:, :inner_half]) * projection[:, inner_half:]).astype(
        jnp.bfloat16
    )
    return jnp.dot(activated, weight_out, preferred_element_type=jnp.float32).astype(jnp.bfloat16)


def local(
    residual,
    queries,
    key_vectors,
    value_vectors,
    output_weight,
    norm_gain,
    routes,
    gate_levels,
    expert_in,
    expert_out,
):
    context_size = lax.axis_size("context")
    expert_size = lax.axis_size("expert")
    tok_rows, width = residual.shape
    head_count = queries.shape[1] // HD
    key_head_count = key_vectors.shape[1] // HD
    group_size = head_count // key_head_count
    heads_here = head_count // context_size
    keys_here = max(1, heads_here // group_size)
    queries_per_key = min(heads_here, group_size)
    group_rows = tok_rows * context_size
    weight_in = expert_in[0]
    weight_out = expert_out[0]
    head_table = (
        (
            np.arange(context_size)[:, None] * heads_here // group_size
            + np.arange(keys_here)[None, :]
        )
        .reshape(-1)
        .astype(np.int32)
    )
    key_select = key_vectors.reshape(tok_rows, key_head_count, HD)[:, head_table].reshape(
        tok_rows, context_size * keys_here * HD
    )
    value_select = value_vectors.reshape(tok_rows, key_head_count, HD)[:, head_table].reshape(
        tok_rows, context_size * keys_here * HD
    )
    query_local, key_local, value_local = (
        lax.all_to_all(queries, "context", split_axis=1, concat_axis=0, tiled=True),
        lax.all_to_all(key_select, "context", split_axis=1, concat_axis=0, tiled=True),
        lax.all_to_all(value_select, "context", split_axis=1, concat_axis=0, tiled=True),
    )
    own_block = lax.axis_index("expert")
    scaling = 1.0 / math.sqrt(HD)
    to_count = query_local.shape[0]
    query_sets = [
        (
            query_local.reshape(to_count, keys_here, queries_per_key, HD)
            .transpose(1, 0, 2, 3)
            .reshape(keys_here, to_count * queries_per_key, HD),
            own_block * group_rows
            + jnp.arange(group_rows * queries_per_key, dtype=jnp.int32) // queries_per_key,
            (own_block + 1) * group_rows,
        )
    ]
    set_counts = [group_rows]
    initial = tuple(
        (
            (
                jnp.full((keys_here, count * queries_per_key), -1e30, jnp.float32),
                jnp.zeros((keys_here, count * queries_per_key), jnp.float32),
                jnp.zeros((keys_here, count * queries_per_key, HD), jnp.float32),
            )
            for count in set_counts
        )
    )
    start = jnp.int32(0)
    key_piece = lax.all_gather(key_local, "expert", axis=0, tiled=True)
    value_piece = lax.all_gather(value_local, "expert", axis=0, tiled=True)
    piece_rows = key_piece.shape[0]
    key_heads = key_piece.reshape(piece_rows, keys_here, HD).transpose(1, 0, 2)
    value_heads = value_piece.reshape(piece_rows, keys_here, HD).transpose(1, 0, 2)
    key_position = jnp.arange(piece_rows, dtype=jnp.int32)
    updated = []
    for query_set, state in zip(query_sets, initial):
        query_rows, query_position, key_limit = query_set

        def update(inner, query_rows=query_rows, query_position=query_position):
            run_max, run_total, accum = inner
            allowed = (key_position[None, :] <= query_position[:, None])[None]
            scores = (
                jnp.einsum(
                    "grd,gnd->grn", query_rows, key_heads, preferred_element_type=jnp.float32
                )
                * scaling
            )
            masked = jnp.where(allowed, scores, -1e30)
            new_max = jnp.maximum(run_max, jnp.max(masked, axis=2))
            weights = jnp.where(allowed, jnp.exp(masked - new_max[:, :, None]), 0.0)
            run_total = jnp.sum(weights, axis=2)
            accum = jnp.einsum(
                "grn,gnd->grd",
                weights.astype(jnp.bfloat16),
                value_heads,
                preferred_element_type=jnp.float32,
            )
            return (new_max, run_total, accum)

        def unchanged(inner):
            return inner

        updated.append(lax.cond(start < key_limit, update, unchanged, state))
    states = tuple(updated)
    run_max, run_total, accum = states[0]
    result = (accum / run_total[:, :, None]).astype(jnp.bfloat16)
    attention = (
        result.reshape(keys_here, group_rows, queries_per_key, HD)
        .transpose(1, 0, 2, 3)
        .reshape(group_rows, heads_here * HD)
    )
    projected = lax.psum_scatter(
        jnp.dot(attention, output_weight, preferred_element_type=jnp.float32).astype(jnp.bfloat16),
        "context",
        scatter_dimension=0,
        tiled=True,
    ).astype(jnp.float32)
    hidden_state = residual.astype(jnp.float32) + projected
    mean_square = jnp.mean(hidden_state * hidden_state, axis=1, keepdims=True)
    normed = (hidden_state * lax.rsqrt(mean_square + 1e-06) * norm_gain).astype(jnp.bfloat16)
    top_count = routes.shape[1]
    expert_count = expert_size * context_size // 2
    group_experts = expert_size // 2
    capacity = min(tok_rows, max(2, 5 * tok_rows * top_count // (4 * expert_count)))
    slot_count = expert_count * capacity
    flat_routes = routes.reshape(-1)
    expert_hits = (
        flat_routes[:, None] == jnp.arange(expert_count, dtype=jnp.int32)[None, :]
    ).astype(jnp.int32)
    earlier = jnp.cumsum(expert_hits, axis=0) - expert_hits
    target_slot = flat_routes * capacity + jnp.sum(earlier * expert_hits, axis=1)
    placement = (
        target_slot.reshape(tok_rows, top_count)[:, :, None]
        == jnp.arange(slot_count, dtype=jnp.int32)[None, None, :]
    )
    sending = jnp.any(placement, axis=1).astype(jnp.bfloat16)
    outgoing = lax.dot_general(
        sending, normed, (((0,), (0,)), ((), ())), preferred_element_type=jnp.float32
    ).astype(jnp.bfloat16)
    gate_shares = jnp.sum(
        jnp.where(placement, gate_levels[:, :, None].astype(jnp.float32) / 256.0, 0.0), axis=1
    ).astype(jnp.bfloat16)
    arrived = lax.all_to_all(
        outgoing.reshape(context_size, group_experts, capacity, width),
        "context",
        split_axis=0,
        concat_axis=0,
        tiled=True,
    )
    item_count = arrived.shape[2]
    copies = jnp.broadcast_to(
        arrived.transpose(1, 0, 2, 3)[:, None], (group_experts, 2, context_size, item_count, width)
    ).reshape(expert_size, context_size, item_count, width)
    rows_in = lax.all_to_all(copies, "expert", split_axis=0, concat_axis=0, tiled=True)
    partial_out = expert_apply(rows_in.reshape(-1, width), weight_in, weight_out).reshape(
        rows_in.shape
    )
    came_back = lax.all_to_all(partial_out, "expert", split_axis=0, concat_axis=0, tiled=True)
    summed = (
        came_back.reshape(group_experts, 2, context_size, item_count, width)
        .astype(jnp.float32)
        .sum(axis=1)
        .astype(jnp.bfloat16)
    )
    result = summed.transpose(1, 0, 2, 3)
    answers = lax.all_to_all(result, "context", split_axis=0, concat_axis=0, tiled=True)
    moe_sum = jnp.dot(
        gate_shares, answers.reshape(slot_count, width), preferred_element_type=jnp.float32
    )
    return hidden_state + moe_sum


def solution(mesh):
    return jax.shard_map(
        local,
        mesh=mesh,
        in_specs=(
            P(("dp", "expert", "context"), None),
            P(("dp", "expert", "context"), None),
            P(("dp", "expert", "context"), None),
            P(("dp", "expert", "context"), None),
            P("context", None),
            P(),
            P(("dp", "expert", "context"), None),
            P(("dp", "expert", "context"), None),
            P(("context", "expert"), None, None),
            P(("context", "expert"), None, None),
        ),
        out_specs=P(("dp", "expert", "context"), None),
        check_vma=False,
    )
```

profile of v0, /device:TPU:8, one launch (start us, length us, event | category | flops | bytes accessed | tf_op | source)
XLA Modules:
  0.0 555.0 jit_solution(13816407835851833400)
XLA Ops:
  8.6 19.3 %all_to_all.68 = bf16[64,8,128]{2,0,1:T(8,128)(2,1)} all-to-all(bf16[64,8,128]{2,0,1:T(8,128)(2,1)S(1)} %bitcast.70), channel_id=1, replica_groups=mesh['context'=8,'expert'=32,'dp'=2] {'context'}, dimensions={1} | all-to-all | bytes 262144 | tf_op jit(solution)/shard_map/all_to_all | solution.py:60
  29.3 12.1 %all_to_all.69 = bf16[64,8,128]{2,0,1:T(8,128)(2,1)} all-to-all(bf16[64,8,128]{2,0,1:T(8,128)(2,1)S(1)} %bitcast.69), channel_id=1, replica_groups=mesh['context'=8,'expert'=32,'dp'=2] {'context'}, dimensions={1} | all-to-all | bytes 262144 | tf_op jit(solution)/shard_map/all_to_all | solution.py:61
  41.5 1.7 copy.96
  43.2 3.4 all-to-all-start
  46.6 10.3 %all-to-all-done = bf16[64,8,256]{2,0,1:T(8,128)(2,1)S(1)} async-done(((bf16[64,8,256]{2,0,1:T(8,128)(2,1)}), bf16[64,8,256]{2,0,1:T(8,128)(2,1)S(1)}, u32[]{:S(2)}, u32[]{:S(2)}) %all-to-all-start) | async-done | bytes 262176 | tf_op jit(solution)/shard_map/all_to_all | solution.py:59
  57.0 54.5 %all-gather.3.cloned.1.call-done = bf16[16384,128]{1,0:T(8,128)(2,1)} async-done(((bf16[512,128]{1,0:T(8,128)(2,1)}), bf16[16384,128]{1,0:T(8,128)(2,1)}) %all-gather.3.cloned.1.call-update) | async-done | bytes 4194320 | tf_op jit(solution)/shard_map/all_gather | solution.py:88
  111.5 87.7 %all-gather.5.cloned.1.call-done = bf16[16384,128]{1,0:T(8,128)(2,1)} async-done(((bf16[512,128]{1,0:T(8,128)(2,1)}), bf16[16384,128]{1,0:T(8,128)(2,1)}) %all-gather.5.cloned.1.call-update) | async-done | bytes 4194320 | tf_op jit(solution)/shard_map/all_gather | solution.py:89
  199.3 74.4 %conditional.1 = (f32[1,1024]{1,0:T(1,128)S(1)}, f32[1,1024,128]{2,1,0:T(8,128)S(1)}) conditional(s32[]{:T(128)} %convert_element_type.51, () %tuple.19, (s32[16384]{0:T(1024)S(1)}, s32[]{:T(128)}, s32[1024]{0:T(1024)S(1)}, bf16[8,64,256]{2,1,0:T(8,128)(2,1)S(1)}, bf16[16384,128]{1,0:T(8,128)(2,1)}, /*index=5*/bf16[16384,128]{1,0:T(8,128)(2,1)}) %tuple.32), branch_computations={%region_0.1_spmd, %region_1.4_spmd} | conditional | flops 8858378240 | bytes 211267616 | solution.py:122
  199.4 25.7 %fusion = (f32[1024]{0:T(1024)S(1)}, f32[1024,16384]{1,0:T(8,128)}) fusion(s32[16384]{0:T(1024)S(1)} %get-tuple-element.90, s32[1024]{0:T(1024)S(1)} %fusion.8, bf16[1024,128]{1,0:T(8,128)(2,1)S(1)} %reshape.111, bf16[16384,128]{1,0:T(8,128)(2,1)} %get-tuple-element.94), kind=kOutput, calls=%fused_computation.4 | convolution fusion | flops 4362075136 | bytes 71639040 | tf_op jit(solution)/shard_map/cond/branch_1_fun/grd,gnd->grn/dot_general | solution.py:102
  225.2 26.5 %fusion.5 = f32[1,1024,128]{2,1,0:T(8,128)S(1)} fusion(bf16[16384,128]{1,0:T(8,128)(2,1)} %get-tuple-element.95, f32[1024,16384]{1,0:T(8,128)} %get-tuple-element.113, f32[1024]{0:T(1024)S(1)} %broadcast_maximum_fusion, s32[16384]{0:T(1024)S(1)} %get-tuple-element.90, s32[1024]{0:T(1024)S(1)} %fusion.8), kind=kOutput, calls=%fused_computation.8 | convolution fusion | flops 4395630592 | bytes 71901184 | tf_op jit(solution)/shard_map/cond/branch_1_fun/grn,gnd->grd/dot_general | solution.py:111
  251.6 22.1 %fusion.2 = f32[1024]{0:T(1024)S(1)} fusion(f32[1024,16384]{1,0:T(8,128)} %get-tuple-element.113, f32[1024]{0:T(1024)S(1)} %broadcast_maximum_fusion, s32[16384]{0:T(1024)S(1)} %get-tuple-element.90, s32[1024]{0:T(1024)S(1)} %fusion.8), kind=kLoop, calls=%fused_computation.6 | loop fusion | flops 100662272 | bytes 67186688 | tf_op jit(solution)/shard_map/cond/branch_1_fun/reduce_sum | solution.py:110
  274.1 1.4 convolution_convert_fusion.2
  277.2 37.8 %reduce-scatter.2.cloned.1.call-done = bf16[64,1024]{1,0:T(8,128)(2,1)} async-done(((bf16[512,1024]{1,0:T(8,128)(2,1)}), bf16[64,1024]{1,0:T(8,128)(2,1)}) %reduce-scatter.2.cloned.1.call-update) | async-done | bytes 131088 | tf_op jit(solution)/shard_map/reduce_scatter | solution.py:131
  315.0 1.0 multiply_reduce_fusion
  316.1 2.5 convolution_convert_fusion.1
  318.7 2.6 reshape.124
  321.3 0.9 copy.81
  322.2 34.2 %all_to_all.70 = bf16[8,16,5,1024]{3,1,2,0:T(8,128)(2,1)S(1)} all-to-all(bf16[8,16,5,1024]{3,1,2,0:T(8,128)(2,1)S(1)} %copy.81), channel_id=1, replica_groups=mesh['context'=8,'expert'=32,'dp'=2] {'context'}, dimensions={0} | all-to-all | bytes 2621440 | tf_op jit(solution)/shard_map/all_to_all | solution.py:162
  357.4 66.3 %all_to_all.71 = bf16[32,8,5,1024]{3,1,2,0:T(8,128)(2,1)S(1)} all-to-all(bf16[32,8,5,1024]{3,1,2,0:T(8,128)(2,1)S(1)} %bitcast.61), channel_id=1, replica_groups=mesh['context'=8,'expert'=32,'dp'=2] {'expert'}, dimensions={0} | all-to-all | bytes 5242880 | tf_op jit(solution)/shard_map/all_to_all | solution.py:173
  423.7 4.0 copy.83
  427.7 4.9 reshape.126
  432.7 1.3 fusion.15
  433.9 0.9 convolution_convert_fusion
  434.8 2.9 reshape.127
  437.7 4.9 copy.84
  442.6 61.2 %all_to_all.72 = bf16[32,8,5,1024]{3,1,2,0:T(8,128)(2,1)S(1)} all-to-all(bf16[32,8,5,1024]{3,1,2,0:T(8,128)(2,1)S(1)} %copy.84), channel_id=1, replica_groups=mesh['context'=8,'expert'=32,'dp'=2] {'expert'}, dimensions={0} | all-to-all | bytes 5242880 | tf_op jit(solution)/shard_map/all_to_all | solution.py:177
  504.4 1.8 copy.86
  506.2 6.4 %all-to-all-start.6 = ((bf16[8,16,5,1024]{3,1,2,0:T(8,128)(2,1)}), bf16[8,16,5,1024]{3,1,2,0:T(8,128)(2,1)}, u32[]{:S(2)}, u32[]{:S(2)}) async-start(bf16[8,16,5,1024]{3,1,2,0:T(8,128)(2,1)} %copy.86), calls=%async_computation.7 | async-start | bytes 2621440 | tf_op jit(solution)/shard_map/all_to_all | solution.py:185
  513.2 29.2 %all-to-all-done.6 = bf16[8,16,5,1024]{3,1,2,0:T(8,128)(2,1)} async-done(((bf16[8,16,5,1024]{3,1,2,0:T(8,128)(2,1)}), bf16[8,16,5,1024]{3,1,2,0:T(8,128)(2,1)}, u32[]{:S(2)}, u32[]{:S(2)}) %all-to-all-start.6) | async-done | bytes 1310752 | tf_op jit(solution)/shard_map/all_to_all | solution.py:185
  542.4 2.2 copy.87
  544.6 1.4 reshape.129
  546.1 2.4 convolution_add_fusion
  (62 shorter events, 7.8 us)
Async XLA Ops:
  6.5 426.1 %copy-start = (bf16[1,1024,384]{2,1,0:T(8,128)(2,1)S(1)}, bf16[1,1024,384]{2,1,0:T(8,128)(2,1)}, u32[]{:S(2)}) copy-start(bf16[1,1024,384]{2,1,0:T(8,128)(2,1)} %param.23) | copy-start | bytes 2359300
  6.5 105.0 %all-gather.3.cloned.1.call-start = ((), (), s32[]{:S(2)}) async-start(), calls=%async_computation.8 | async-start | bytes 4325376 | tf_op jit(solution)/shard_map/all_gather | solution.py:88
  28.0 171.3 %all-gather.5.cloned.1.call-start = ((), (), s32[]{:S(2)}) async-start(), calls=%async_computation.9 | async-start | bytes 4325376 | tf_op jit(solution)/shard_map/all_gather | solution.py:89
  43.2 13.8 %all-to-all-start = ((bf16[64,8,256]{2,0,1:T(8,128)(2,1)}), bf16[64,8,256]{2,0,1:T(8,128)(2,1)S(1)}, u32[]{:S(2)}, u32[]{:S(2)}) async-start(bf16[64,8,256]{2,0,1:T(8,128)(2,1)} %bitcast.57), calls=%async_computation | async-start | bytes 524288 | tf_op jit(solution)/shard_map/all_to_all | solution.py:59
  46.6 268.4 %reduce-scatter.2.cloned.1.call-start = ((), (), s32[]{:S(2)}) async-start(), calls=%async_computation.10 | async-start | bytes 1179648 | tf_op jit(solution)/shard_map/reduce_scatter | solution.py:131
  199.3 74.8 %copy-start.3 = (bf16[256,1024]{1,0:T(8,128)(2,1)S(1)}, bf16[256,1024]{1,0:T(8,128)(2,1)}, u32[]{:S(2)}) copy-start(bf16[256,1024]{1,0:T(8,128)(2,1)} %param.19) | copy-start | bytes 1572868
  273.7 1.8 copy-start.6
  273.7 41.3 %copy-start.1 = (bf16[64,1024]{1,0:T(8,128)(2,1)S(1)}, bf16[64,1024]{1,0:T(8,128)(2,1)}, u32[]{:S(2)}) copy-start(bf16[64,1024]{1,0:T(8,128)(2,1)} %param.15) | copy-start | bytes 393220
  273.7 42.4 %copy-start.7 = (f32[1024]{0:T(1024)S(1)}, f32[1024]{0:T(1024)}, u32[]{:S(2)}) copy-start(f32[1024]{0:T(1024)} %param.20) | copy-start | bytes 12292
  276.7 39.4 %copy-start.4 = (s32[64,8]{1,0:T(8,128)}, s32[64,8]{1,0:T(8,128)S(1)}, u32[]{:S(2)}) copy-start(s32[64,8]{1,0:T(8,128)S(1)} %copy.79) | copy-start | bytes 6148
  432.6 1.3 copy-start.9
  503.8 8.8 %copy-start.8 = (s32[64,8]{0,1:T(8,128)S(1)}, s32[64,8]{0,1:T(8,128)}, u32[]{:S(2)}) copy-start(s32[64,8]{0,1:T(8,128)} %param.22) | copy-start | bytes 6148
  503.8 8.9 %copy-start.5 = (s32[64,8]{1,0:T(8,128)S(1)}, s32[64,8]{1,0:T(8,128)}, u32[]{:S(2)}) copy-start(s32[64,8]{1,0:T(8,128)} %copy-done.4) | copy-start | bytes 6148
  506.2 39.9 %copy-start.2 = (bf16[64,1024]{1,0:T(8,128)(2,1)S(1)}, bf16[64,1024]{1,0:T(8,128)(2,1)}, u32[]{:S(2)}) copy-start(bf16[64,1024]{1,0:T(8,128)(2,1)} %reduce-scatter.2.cloned.1.call-done) | copy-start | bytes 393220
  506.2 36.2 %all-to-all-start.6 = ((bf16[8,16,5,1024]{3,1,2,0:T(8,128)(2,1)}), bf16[8,16,5,1024]{3,1,2,0:T(8,128)(2,1)}, u32[]{:S(2)}, u32[]{:S(2)}) async-start(bf16[8,16,5,1024]{3,1,2,0:T(8,128)(2,1)} %copy.86), calls=%async_computation.7 | async-start | bytes 2621440 | tf_op jit(solution)/shard_map/all_to_all | solution.py:185
Sparse Core Ops, SparseCore 0:
  28.1 83.4 all-gather.2
  114.7 84.5 all-gather.4
  275.7 39.3 reduce-scatter.1
where the time goes:
time: 556 us; the launch traced here: 555 us
  waiting for transfers between devices  220 us (40%)
  blocking collectives  193 us (35%)
  matrix products  60.7 us (11%)
  local copies, waits for them, and re-layouts  32 us (6%)
  other arithmetic  26.1 us (5%)
  between operations  13.4 us (2%)
  starting transfers between devices  9.92 us (2%)
    all_gather x1, waiting for transfers between devices, local(): value_piece = lax.all_gather(value_local, 'expert', axis=0, tiled=True)  87.7 us
    all_to_all x1, blocking collectives, local(): lax.all_to_all(copies, 'expert', split_axis=0, concat_axis=0, tiled=True)  66.3 us
    all_to_all x1, blocking collectives, local(): lax.all_to_all(partial_out, 'expert', split_axis=0, concat_axis=0, tiled=...  61.2 us
    all_gather x1, waiting for transfers between devices, local(): key_piece = lax.all_gather(key_local, 'expert', axis=0, tiled=True)  54.5 us
    reduce_scatter x1, waiting for transfers between devices, local(): lax.psum_scatter(jnp.dot(attention, output_weight, preferred_element_type...  37.8 us
    all_to_all x1, blocking collectives, local(): lax.all_to_all(outgoing.reshape(context_size, group_experts, capacity, wi...  34.2 us
    all_to_all x1, waiting for transfers between devices, local(): lax.all_to_all(result, 'context', split_axis=0, concat_axis=0, tiled=True)  29.2 us
    dot_general x1, matrix products, update(): jnp.einsum('grn,gnd->grd', weights.astype(jnp.bfloat16), value_heads, pre...  26.5 us
  transfers between devices with their start and end apart: 5, of which 5 were waited for; matrix products, arithmetic and copies ran while one was open for 1% of the time, Pallas kernels for 0%

commit v1 on v0

--- a/solution.py
+++ b/solution.py
@@ -6,6 +6,29 @@
 from jax.sharding import PartitionSpec as P
 
 HD = 128
+
+
+def cut_along(x, dim, count):
+    shape = x.shape
+    blocks = x.reshape(*shape[:dim], count, shape[dim] // count, *shape[dim + 1 :])
+    return jnp.moveaxis(blocks, dim, 0)
+
+
+def laid_out(blocks, dim):
+    dims = list(blocks.shape[1:])
+    dims[dim] *= blocks.shape[0]
+    return jnp.moveaxis(blocks, 0, dim).reshape(dims)
+
+
+def pairwise_exchange(array, axis, split_dim, concat_dim):
+    size, index = (lax.axis_size(axis), lax.axis_index(axis))
+    tiles = cut_along(array, split_dim, size)
+    outs = [tiles[index]]
+    for step in range(1, size):
+        sent = tiles[index ^ step]
+        outs.append(lax.ppermute(sent, axis, [(i, i ^ step) for i in range(size)]))
+    tiles = jnp.stack(outs)[index ^ jnp.arange(size)]
+    return laid_out(tiles, concat_dim)
 
 
 def expert_apply(gathered, weight_in, weight_out):
@@ -57,7 +80,7 @@
     )
     query_local, key_local, value_local = (
         lax.all_to_all(queries, "context", split_axis=1, concat_axis=0, tiled=True),
-        lax.all_to_all(key_select, "context", split_axis=1, concat_axis=0, tiled=True),
+        pairwise_exchange(key_select, "context", 1, 0),
         lax.all_to_all(value_select, "context", split_axis=1, concat_axis=0, tiled=True),
     )
     own_block = lax.axis_index("expert")

time: 556 us -> 576 us (1.036)
  starting transfers between devices: 9.92 us -> 42.3 us
  blocking collectives: 193 us -> 174 us
  waiting for transfers between devices: 220 us -> 226 us
    ppermute x0 -> x7, starting transfers between devices: none -> 32.7 us  [pairwise_exchange(): outs.append(lax.ppermute(sent, axis, [(i, i ^ step) for i in range(size)]))]
    all_to_all x1 -> x0, blocking collectives: 19.3 us -> none  [local(): lax.all_to_all(key_select, 'context', split_axis=1, concat_axis=0, tiled=...]
  transfers between devices with their start and end apart: 5 -> 12, of which waited for: 5 -> 6; matrix products, arithmetic and copies ran while one was open for 1% -> 1% of each run, Pallas kernels for 0% -> 0%
where the time goes in v1:
time: 576 us; the launch traced here: 575 us
  waiting for transfers between devices  226 us (39%)
  blocking collectives  174 us (30%)
  matrix products  60.6 us (11%)
  starting transfers between devices  42.3 us (7%)
  local copies, waits for them, and re-layouts  33.2 us (6%)
  other arithmetic  26.1 us (5%)
  between operations  13.5 us (2%)
    all_gather x1, waiting for transfers between devices, local(): value_piece = lax.all_gather(value_local, 'expert', axis=0, tiled=True)  87.7 us
    all_to_all x1, blocking collectives, local(): lax.all_to_all(copies, 'expert', split_axis=0, concat_axis=0, tiled=True)  66.3 us
    all_to_all x1, blocking collectives, local(): lax.all_to_all(partial_out, 'expert', split_axis=0, concat_axis=0, tiled=...  61.1 us
    all_gather x1, waiting for transfers between devices, local(): key_piece = lax.all_gather(key_local, 'expert', axis=0, tiled=True)  55.5 us
    reduce_scatter x1, waiting for transfers between devices, local(): lax.psum_scatter(jnp.dot(attention, output_weight, preferred_element_type...  38 us
    all_to_all x1, blocking collectives, local(): lax.all_to_all(outgoing.reshape(context_size, group_experts, capacity, wi...  34.1 us
    ppermute x7, starting transfers between devices, pairwise_exchange(): outs.append(lax.ppermute(sent, axis, [(i, i ^ step) for i in range(size)]))  32.7 us
    all_to_all x1, waiting for transfers between devices, local(): lax.all_to_all(result, 'context', split_axis=0, concat_axis=0, tiled=True)  29 us
  transfers between devices with their start and end apart: 12, of which 6 were waited for; matrix products, arithmetic and copies ran while one was open for 1% of the time, Pallas kernels for 0%

profile of v1, /device:TPU:8, one launch (start us, length us, event | category | flops | bytes accessed | tf_op | source)
XLA Modules:
  0.0 575.1 jit_solution(10097242134969723054)
XLA Ops:
  8.7 4.3 collective-permute-start
  12.9 6.1 %collective-permute-start.1 = (bf16[64,128]{1,0:T(8,128)(2,1)S(1)}, bf16[64,128]{1,0:T(8,128)(2,1)S(1)}, u32[]{:S(2)}, u32[]{:S(2)}) collective-permute-start(bf16[64,128]{1,0:T(8,128)(2,1)S(1)} %get-tuple-element.119), channel_id=1, source_target_pairs={{0,128},{64,192},{128,0},{192,64},{256,384},{320,448},{384,256},{4... | collective-permute-start | bytes 49160 | tf_op jit(solution)/shard_map/ppermute | solution.py:29
  19.0 1.9 collective-permute-start.2
  21.0 8.7 %collective-permute-start.3 = (bf16[64,128]{1,0:T(8,128)(2,1)S(1)}, bf16[64,128]{1,0:T(8,128)(2,1)S(1)}, u32[]{:S(2)}, u32[]{:S(2)}) collective-permute-start(bf16[64,128]{1,0:T(8,128)(2,1)S(1)} %get-tuple-element.117), channel_id=1, source_target_pairs={{0,256},{64,320},{128,384},{192,448},{256,0},{320,64},{384,128},{4... | collective-permute-start | bytes 49160 | tf_op jit(solution)/shard_map/ppermute | solution.py:29
  29.7 1.9 collective-permute-start.4
  31.7 7.9 %collective-permute-start.5 = (bf16[64,128]{1,0:T(8,128)(2,1)S(1)}, bf16[64,128]{1,0:T(8,128)(2,1)S(1)}, u32[]{:S(2)}, u32[]{:S(2)}) collective-permute-start(bf16[64,128]{1,0:T(8,128)(2,1)S(1)} %get-tuple-element.115), channel_id=1, source_target_pairs={{0,384},{64,448},{128,256},{192,320},{256,128},{320,192},{384,0},{... | collective-permute-start | bytes 49160 | tf_op jit(solution)/shard_map/ppermute | solution.py:29
  39.6 1.9 collective-permute-start.6
  41.6 5.0 collective-permute-done.6
  49.2 12.1 %all_to_all.52 = bf16[64,8,128]{2,0,1:T(8,128)(2,1)} all-to-all(bf16[64,8,128]{2,0,1:T(8,128)(2,1)S(1)} %bitcast.96), channel_id=1, replica_groups=mesh['context'=8,'expert'=32,'dp'=2] {'context'}, dimensions={1} | all-to-all | bytes 262144 | tf_op jit(solution)/shard_map/all_to_all | solution.py:84
  63.0 3.4 all-to-all-start
  66.5 10.3 %all-to-all-done = bf16[64,8,256]{2,0,1:T(8,128)(2,1)S(1)} async-done(((bf16[64,8,256]{2,0,1:T(8,128)(2,1)}), bf16[64,8,256]{2,0,1:T(8,128)(2,1)S(1)}, u32[]{:S(2)}, u32[]{:S(2)}) %all-to-all-start) | async-done | bytes 262176 | tf_op jit(solution)/shard_map/all_to_all | solution.py:82
  76.9 55.5 %all-gather.3.cloned.1.call-done = bf16[16384,128]{1,0:T(8,128)(2,1)} async-done(((bf16[512,128]{1,0:T(8,128)(2,1)}), bf16[16384,128]{1,0:T(8,128)(2,1)}) %all-gather.3.cloned.1.call-update) | async-done | bytes 4194320 | tf_op jit(solution)/shard_map/all_gather | solution.py:111
  132.4 87.7 %all-gather.5.cloned.1.call-done = bf16[16384,128]{1,0:T(8,128)(2,1)} async-done(((bf16[512,128]{1,0:T(8,128)(2,1)}), bf16[16384,128]{1,0:T(8,128)(2,1)}) %all-gather.5.cloned.1.call-update) | async-done | bytes 4194320 | tf_op jit(solution)/shard_map/all_gather | solution.py:112
  220.2 74.3 %conditional.1 = (f32[1,1024]{1,0:T(1,128)S(1)}, f32[1,1024,128]{2,1,0:T(8,128)S(1)}) conditional(s32[]{:T(128)} %convert_element_type.51, () %tuple.19, (s32[16384]{0:T(1024)S(1)}, s32[]{:T(128)}, s32[1024]{0:T(1024)S(1)}, bf16[8,64,256]{2,1,0:T(8,128)(2,1)S(1)}, bf16[16384,128]{1,0:T(8,128)(2,1)}, /*index=5*/bf16[16384,128]{1,0:T(8,128)(2,1)}) %tuple.39), branch_computations={%region_0.1_spmd, %region_1.4_spmd} | conditional | flops 8858378240 | bytes 211267616 | solution.py:145
  220.3 25.7 %fusion = (f32[1024]{0:T(1024)S(1)}, f32[1024,16384]{1,0:T(8,128)}) fusion(s32[16384]{0:T(1024)S(1)} %get-tuple-element.90, s32[1024]{0:T(1024)S(1)} %fusion.8, bf16[1024,128]{1,0:T(8,128)(2,1)S(1)} %reshape.139, bf16[16384,128]{1,0:T(8,128)(2,1)} %get-tuple-element.94), kind=kOutput, calls=%fused_computation.5 | convolution fusion | flops 4362075136 | bytes 71639040 | tf_op jit(solution)/shard_map/cond/branch_1_fun/grd,gnd->grn/dot_general | solution.py:125
  246.0 26.5 %fusion.5 = f32[1,1024,128]{2,1,0:T(8,128)S(1)} fusion(bf16[16384,128]{1,0:T(8,128)(2,1)} %get-tuple-element.95, f32[1024,16384]{1,0:T(8,128)} %get-tuple-element.113, f32[1024]{0:T(1024)S(1)} %broadcast_maximum_fusion, s32[16384]{0:T(1024)S(1)} %get-tuple-element.90, s32[1024]{0:T(1024)S(1)} %fusion.8), kind=kOutput, calls=%fused_computation.9 | convolution fusion | flops 4395630592 | bytes 71901184 | tf_op jit(solution)/shard_map/cond/branch_1_fun/grn,gnd->grd/dot_general | solution.py:134
  272.4 22.1 %fusion.2 = f32[1024]{0:T(1024)S(1)} fusion(f32[1024,16384]{1,0:T(8,128)} %get-tuple-element.113, f32[1024]{0:T(1024)S(1)} %broadcast_maximum_fusion, s32[16384]{0:T(1024)S(1)} %get-tuple-element.90, s32[1024]{0:T(1024)S(1)} %fusion.8), kind=kLoop, calls=%fused_computation.7 | loop fusion | flops 100662272 | bytes 67186688 | tf_op jit(solution)/shard_map/cond/branch_1_fun/reduce_sum | solution.py:133
  298.0 38.0 %reduce-scatter.2.cloned.1.call-done = bf16[64,1024]{1,0:T(8,128)(2,1)} async-done(((bf16[512,1024]{1,0:T(8,128)(2,1)}), bf16[64,1024]{1,0:T(8,128)(2,1)}) %reduce-scatter.2.cloned.1.call-update) | async-done | bytes 131088 | tf_op jit(solution)/shard_map/reduce_scatter | solution.py:154
  337.0 2.6 convolution_convert_fusion.1
  339.6 2.6 reshape.154
  343.1 34.1 %all_to_all.53 = bf16[8,16,5,1024]{3,1,2,0:T(8,128)(2,1)S(1)} all-to-all(bf16[8,16,5,1024]{3,1,2,0:T(8,128)(2,1)S(1)} %copy.81), channel_id=1, replica_groups=mesh['context'=8,'expert'=32,'dp'=2] {'context'}, dimensions={0} | all-to-all | bytes 2621440 | tf_op jit(solution)/shard_map/all_to_all | solution.py:185
  378.3 66.3 %all_to_all.54 = bf16[32,8,5,1024]{3,1,2,0:T(8,128)(2,1)S(1)} all-to-all(bf16[32,8,5,1024]{3,1,2,0:T(8,128)(2,1)S(1)} %bitcast.88), channel_id=1, replica_groups=mesh['context'=8,'expert'=32,'dp'=2] {'expert'}, dimensions={0} | all-to-all | bytes 5242880 | tf_op jit(solution)/shard_map/all_to_all | solution.py:196
  444.5 4.0 copy.83
  448.6 4.9 reshape.156
  455.7 2.8 reshape.157
  458.5 4.9 copy.84
  463.4 61.1 %all_to_all.55 = bf16[32,8,5,1024]{3,1,2,0:T(8,128)(2,1)S(1)} all-to-all(bf16[32,8,5,1024]{3,1,2,0:T(8,128)(2,1)S(1)} %copy.84), channel_id=1, replica_groups=mesh['context'=8,'expert'=32,'dp'=2] {'expert'}, dimensions={0} | all-to-all | bytes 5242880 | tf_op jit(solution)/shard_map/all_to_all | solution.py:200
  525.1 1.8 copy.86
  526.9 6.0 %all-to-all-start.5 = ((bf16[8,16,5,1024]{3,1,2,0:T(8,128)(2,1)}), bf16[8,16,5,1024]{3,1,2,0:T(8,128)(2,1)}, u32[]{:S(2)}, u32[]{:S(2)}) async-start(bf16[8,16,5,1024]{3,1,2,0:T(8,128)(2,1)} %copy.86), calls=%async_computation.6 | async-start | bytes 2621440 | tf_op jit(solution)/shard_map/all_to_all | solution.py:208
  533.5 29.0 %all-to-all-done.5 = bf16[8,16,5,1024]{3,1,2,0:T(8,128)(2,1)} async-done(((bf16[8,16,5,1024]{3,1,2,0:T(8,128)(2,1)}), bf16[8,16,5,1024]{3,1,2,0:T(8,128)(2,1)}, u32[]{:S(2)}, u32[]{:S(2)}) %all-to-all-start.5) | async-done | bytes 1310752 | tf_op jit(solution)/shard_map/all_to_all | solution.py:208
  562.6 2.2 copy.87
  566.2 2.4 convolution_add_fusion
  (86 shorter events, 17.7 us)
Async XLA Ops:
  6.5 446.9 %copy-start = (bf16[1,1024,384]{2,1,0:T(8,128)(2,1)S(1)}, bf16[1,1024,384]{2,1,0:T(8,128)(2,1)}, u32[]{:S(2)}) copy-start(bf16[1,1024,384]{2,1,0:T(8,128)(2,1)} %param.23) | copy-start | bytes 2359300
  6.5 125.9 %all-gather.3.cloned.1.call-start = ((), (), s32[]{:S(2)}) async-start(), calls=%async_computation.7 | async-start | bytes 4325376 | tf_op jit(solution)/shard_map/all_gather | solution.py:111
  8.7 23.0 %collective-permute-start = (bf16[64,128]{1,0:T(8,128)(2,1)S(1)}, bf16[64,128]{1,0:T(8,128)(2,1)S(1)}, u32[]{:S(2)}, u32[]{:S(2)}) collective-permute-start(bf16[64,128]{1,0:T(8,128)(2,1)S(1)} %get-tuple-element.120), channel_id=1, source_target_pairs={{0,64},{64,0},{128,192},{192,128},{256,320},{320,256},{384,448},{4... | collective-permute-start | bytes 49160 | tf_op jit(solution)/shard_map/ppermute | solution.py:29
  12.9 26.6 %collective-permute-start.1 = (bf16[64,128]{1,0:T(8,128)(2,1)S(1)}, bf16[64,128]{1,0:T(8,128)(2,1)S(1)}, u32[]{:S(2)}, u32[]{:S(2)}) collective-permute-start(bf16[64,128]{1,0:T(8,128)(2,1)S(1)} %get-tuple-element.119), channel_id=1, source_target_pairs={{0,128},{64,192},{128,0},{192,64},{256,384},{320,448},{384,256},{4... | collective-permute-start | bytes 49160 | tf_op jit(solution)/shard_map/ppermute | solution.py:29
  19.0 22.5 %collective-permute-start.2 = (bf16[64,128]{1,0:T(8,128)(2,1)S(1)}, bf16[64,128]{1,0:T(8,128)(2,1)S(1)}, u32[]{:S(2)}, u32[]{:S(2)}) collective-permute-start(bf16[64,128]{1,0:T(8,128)(2,1)S(1)} %get-tuple-element.118), channel_id=1, source_target_pairs={{0,192},{64,128},{128,64},{192,0},{256,448},{320,384},{384,320},{4... | collective-permute-start | bytes 49160 | tf_op jit(solution)/shard_map/ppermute | solution.py:29
  21.0 20.6 %collective-permute-start.3 = (bf16[64,128]{1,0:T(8,128)(2,1)S(1)}, bf16[64,128]{1,0:T(8,128)(2,1)S(1)}, u32[]{:S(2)}, u32[]{:S(2)}) collective-permute-start(bf16[64,128]{1,0:T(8,128)(2,1)S(1)} %get-tuple-element.117), channel_id=1, source_target_pairs={{0,256},{64,320},{128,384},{192,448},{256,0},{320,64},{384,128},{4... | collective-permute-start | bytes 49160 | tf_op jit(solution)/shard_map/ppermute | solution.py:29
  29.7 11.8 %collective-permute-start.4 = (bf16[64,128]{1,0:T(8,128)(2,1)S(1)}, bf16[64,128]{1,0:T(8,128)(2,1)S(1)}, u32[]{:S(2)}, u32[]{:S(2)}) collective-permute-start(bf16[64,128]{1,0:T(8,128)(2,1)S(1)} %get-tuple-element.116), channel_id=1, source_target_pairs={{0,320},{64,256},{128,448},{192,384},{256,64},{320,0},{384,192},{4... | collective-permute-start | bytes 49160 | tf_op jit(solution)/shard_map/ppermute | solution.py:29
  31.7 9.9 %collective-permute-start.5 = (bf16[64,128]{1,0:T(8,128)(2,1)S(1)}, bf16[64,128]{1,0:T(8,128)(2,1)S(1)}, u32[]{:S(2)}, u32[]{:S(2)}) collective-permute-start(bf16[64,128]{1,0:T(8,128)(2,1)S(1)} %get-tuple-element.115), channel_id=1, source_target_pairs={{0,384},{64,448},{128,256},{192,320},{256,128},{320,192},{384,0},{... | collective-permute-start | bytes 49160 | tf_op jit(solution)/shard_map/ppermute | solution.py:29
  39.6 7.0 %collective-permute-start.6 = (bf16[64,128]{1,0:T(8,128)(2,1)S(1)}, bf16[64,128]{1,0:T(8,128)(2,1)S(1)}, u32[]{:S(2)}, u32[]{:S(2)}) collective-permute-start(bf16[64,128]{1,0:T(8,128)(2,1)S(1)} %get-tuple-element.114), channel_id=1, source_target_pairs={{0,448},{64,384},{128,320},{192,256},{256,192},{320,128},{384,64},... | collective-permute-start | bytes 49160 | tf_op jit(solution)/shard_map/ppermute | solution.py:29
  47.8 172.3 %all-gather.5.cloned.1.call-start = ((), (), s32[]{:S(2)}) async-start(), calls=%async_computation.8 | async-start | bytes 4325376 | tf_op jit(solution)/shard_map/all_gather | solution.py:112
  63.0 13.8 %all-to-all-start = ((bf16[64,8,256]{2,0,1:T(8,128)(2,1)}), bf16[64,8,256]{2,0,1:T(8,128)(2,1)S(1)}, u32[]{:S(2)}, u32[]{:S(2)}) async-start(bf16[64,8,256]{2,0,1:T(8,128)(2,1)} %bitcast.84), calls=%async_computation | async-start | bytes 524288 | tf_op jit(solution)/shard_map/all_to_all | solution.py:82
  66.5 269.5 %reduce-scatter.2.cloned.1.call-start = ((), (), s32[]{:S(2)}) async-start(), calls=%async_computation.9 | async-start | bytes 1179648 | tf_op jit(solution)/shard_map/reduce_scatter | solution.py:154
  220.1 74.7 %copy-start.3 = (bf16[256,1024]{1,0:T(8,128)(2,1)S(1)}, bf16[256,1024]{1,0:T(8,128)(2,1)}, u32[]{:S(2)}) copy-start(bf16[256,1024]{1,0:T(8,128)(2,1)} %param.19) | copy-start | bytes 1572868
  294.5 1.8 copy-start.6
  294.5 41.4 %copy-start.1 = (bf16[64,1024]{1,0:T(8,128)(2,1)S(1)}, bf16[64,1024]{1,0:T(8,128)(2,1)}, u32[]{:S(2)}) copy-start(bf16[64,1024]{1,0:T(8,128)(2,1)} %param.15) | copy-start | bytes 393220
  294.5 42.5 %copy-start.7 = (f32[1024]{0:T(1024)S(1)}, f32[1024]{0:T(1024)}, u32[]{:S(2)}) copy-start(f32[1024]{0:T(1024)} %param.20) | copy-start | bytes 12292
  297.5 39.5 %copy-start.4 = (s32[64,8]{1,0:T(8,128)}, s32[64,8]{1,0:T(8,128)S(1)}, u32[]{:S(2)}) copy-start(s32[64,8]{1,0:T(8,128)S(1)} %copy.79) | copy-start | bytes 6148
  453.5 1.3 copy-start.9
  524.5 8.4 %copy-start.8 = (s32[64,8]{0,1:T(8,128)S(1)}, s32[64,8]{0,1:T(8,128)}, u32[]{:S(2)}) copy-start(s32[64,8]{0,1:T(8,128)} %param.22) | copy-start | bytes 6148
  524.5 8.5 %copy-start.5 = (s32[64,8]{1,0:T(8,128)S(1)}, s32[64,8]{1,0:T(8,128)}, u32[]{:S(2)}) copy-start(s32[64,8]{1,0:T(8,128)} %copy-done.4) | copy-start | bytes 6148
  526.9 39.3 %copy-start.2 = (bf16[64,1024]{1,0:T(8,128)(2,1)S(1)}, bf16[64,1024]{1,0:T(8,128)(2,1)}, u32[]{:S(2)}) copy-start(bf16[64,1024]{1,0:T(8,128)(2,1)} %reduce-scatter.2.cloned.1.call-done) | copy-start | bytes 393220
  526.9 35.7 %all-to-all-start.5 = ((bf16[8,16,5,1024]{3,1,2,0:T(8,128)(2,1)}), bf16[8,16,5,1024]{3,1,2,0:T(8,128)(2,1)}, u32[]{:S(2)}, u32[]{:S(2)}) async-start(bf16[8,16,5,1024]{3,1,2,0:T(8,128)(2,1)} %copy.86), calls=%async_computation.6 | async-start | bytes 2621440 | tf_op jit(solution)/shard_map/all_to_all | solution.py:208
Sparse Core Ops, SparseCore 0:
  47.9 84.4 all-gather.2
  135.6 84.5 all-gather.4
  296.4 39.4 reduce-scatter.1
